TPU v7x, 32 devices: a whole 2x2x4 slice. The times are simulated.
32 devices in a mesh: dp: 8 (over y, x, core), sp: 4 (over z).
Axes of the slice: x: 2, y: 2, z: 4, core: 2. Of those that a mesh axis runs over, the one named last changes fastest.
Arguments:
- inputs: bfloat16 [16, 2048, 768], P('dp', 'sp'), may hold values from -6 to 6
- out_grad: bfloat16 [16, 2048, 768], P('dp', 'sp'), may hold values from -6 to 6
- segment_ids: int32 [16, 2048], P('dp'), may hold values from 0 to 7, as said below
- positions: int32 [16, 2048], P('dp'), may hold values from 0 to 1023, as said below
- norm1_gain: bfloat16 [768], replicated, may hold values from 0.5 to 1.5
- norm1_bias: bfloat16 [768], replicated, may hold values from -1.75 to 1.75
- norm2_gain: bfloat16 [768], replicated, may hold values from 0.5 to 1.5
- norm2_bias: bfloat16 [768], replicated, may hold values from -1.75 to 1.75
- query_weight: bfloat16 [768, 768], replicated, may hold values from -0.21875 to 0.21875
- query_bias: bfloat16 [768], replicated, may hold values from -1.75 to 1.75
- key_weight: bfloat16 [768, 64], replicated, may hold values from -0.21875 to 0.21875
- key_bias: bfloat16 [16], replicated, may hold values from -1.75 to 1.75
- value_weight: bfloat16 [768, 64], replicated, may hold values from -0.21875 to 0.21875
- value_bias: bfloat16 [64], replicated, may hold values from -1.75 to 1.75
- output_weight: bfloat16 [768, 768], replicated, may hold values from -2.5 to 2.5
- output_bias: bfloat16 [768], replicated, may hold values from -1.75 to 1.75
- hidden_weight: bfloat16 [768, 3072], replicated, may hold values from -0.21875 to 0.21875
- hidden_bias: bfloat16 [3072], replicated, may hold values from -1.75 to 1.75
- down_weight: bfloat16 [3072, 768], replicated, may hold values from -0.109375 to 0.109375
- down_bias: bfloat16 [768], replicated, may hold values from -1.75 to 1.75
Outputs:
- layer_out: bfloat16 [16, 2048, 768], P('dp', 'sp')
- input_grad: float32 [16, 2048, 768], P('dp', 'sp')
- norm1_gain_grad: float32 [768], P('sp')
- norm1_bias_grad: float32 [768], P('sp')
- norm2_gain_grad: float32 [768], P('sp')
- norm2_bias_grad: float32 [768], P('sp')
- query_weight_grad: float32 [768, 768], P('sp')
- query_bias_grad: float32 [768], P('sp')
- key_weight_grad: float32 [768, 64], P('sp')
- key_bias_grad: float32 [16], P('sp')
- value_weight_grad: float32 [768, 64], P('sp')
- value_bias_grad: float32 [64], P('sp')
- output_weight_grad: float32 [768, 768], P('sp')
- output_bias_grad: float32 [768], P('sp')
- hidden_weight_grad: float32 [768, 3072], P('sp')
- hidden_bias_grad: float32 [3072], P('sp')
- down_weight_grad: float32 [3072, 768], P('sp')
- down_bias_grad: float32 [768], P('sp')
Inputs may be any that keep to these rules, and one draw needn't show every extreme that they name: `segment_ids`: document numbers of a row start at 0 and rise by one at each of its 7 boundaries, so every row holds exactly 8 documents; the first document of every row holds exactly 1024 tokens and each other document fewer. `positions`: each token's place counted from 0 at the first token of its document.
All inputs are finite; a program needn't handle non-finite values.
Results may differ from a plain program's by a relative error of at most 0.0085.
The roundings to bfloat16 on the way count: a program that leaves them out, or rounds other values in their place, can miss the bound.
Values may be sent and summed in bfloat16 or wider, within the bound.
No kernel may reach another device: no remote copies, remote signals or barrier semaphores. Data moves between devices by JAX's collectives and lax.ppermute only.
A program may use at most 256 MiB of HBM per device.

v0:
```python
import jax
import jax.numpy as jnp
from jax import lax
from jax.sharding import PartitionSpec as P

ROT = 16
EPSILON = 1e-05


def norm_forward(token_rows, gain_vec, offset):
    row_mean = jnp.mean(token_rows, -1, keepdims=True)
    centered = token_rows - row_mean
    inverse = lax.rsqrt(jnp.mean(centered * centered, -1, keepdims=True) + EPSILON)
    normed = centered * inverse
    return (normed * gain_vec + offset, normed, inverse)


def norm_backward(grad_out, normed, inverse, gain_vec):
    scaled = grad_out * gain_vec
    inner_sum = jnp.mean(scaled * normed, -1, keepdims=True)
    grad_in = inverse * (scaled - jnp.mean(scaled, -1, keepdims=True) - normed * inner_sum)
    return (grad_in, jnp.sum(grad_out * normed, 0), jnp.sum(grad_out, 0))


def rope_tables(places):
    half_rot = ROT // 2
    frequency = 10000.0 ** (-(jnp.arange(half_rot, dtype=jnp.float32) * 2.0) / ROT)
    angles = places.astype(jnp.float32)[:, None] * frequency[None, :]
    return (jnp.cos(angles), jnp.sin(angles))


def rotate(values_in, cosine, sine_tab):
    half_rot = ROT // 2
    first_part = values_in[..., :half_rot]
    second_part = values_in[..., half_rot:ROT]
    return jnp.concatenate(
        [
            first_part * cosine - second_part * sine_tab,
            second_part * cosine + first_part * sine_tab,
            values_in[..., ROT:],
        ],
        -1,
    )


def times_transposed(matrix_a, matrix_b):
    return lax.dot_general(
        matrix_a, matrix_b, (((1,), (1,)), ((), ())), preferred_element_type=jnp.float32
    )


def transposed_times(matrix_a, matrix_b):
    return lax.dot_general(
        matrix_a, matrix_b, (((0,), (0,)), ((), ())), preferred_element_type=jnp.float32
    )


def block_mask(seg_query, index_query, segments_all, block_start, block_end, key_end):
    key_index = jnp.arange(key_end, dtype=jnp.int32)
    same_doc = seg_query[block_start:block_end][:, None] == segments_all[None, :key_end]
    earlier = key_index[None, :] <= index_query[block_start:block_end][:, None]
    return (same_doc & earlier)[:, None, :]


def attend_forward(queries, keys_all, values_all, seg_query, index_query, segments_all):
    row_count = queries.shape[0]
    head_dim = keys_all.shape[1]
    heads_here = queries.shape[1] // head_dim
    full_len = keys_all.shape[0]
    block_rows = 512
    scale_factor = head_dim ** (-0.5)
    outputs, lse_list = ([], [])
    for block_start in range(0, row_count, block_rows):
        block_end = block_start + block_rows
        key_end = min(full_len, block_end)
        query_block = queries[block_start:block_end].reshape(block_rows, heads_here, head_dim)
        scores = (
            jnp.einsum(
                "qhd,kd->qhk", query_block, keys_all[:key_end], preferred_element_type=jnp.float32
            )
            * scale_factor
        )
        allowed = block_mask(seg_query, index_query, segments_all, block_start, block_end, key_end)
        masked = jnp.where(allowed, scores, -1e30)
        top_score = jnp.max(masked, -1, keepdims=True)
        exponent = jnp.exp(masked - top_score)
        total_weight = jnp.sum(exponent, -1, keepdims=True)
        weights_blk = (exponent / total_weight).astype(jnp.bfloat16)
        out_block = jnp.einsum(
            "qhk,kd->qhd", weights_blk, values_all[:key_end], preferred_element_type=jnp.float32
        )
        outputs.append(out_block.reshape(block_rows, heads_here * head_dim).astype(jnp.bfloat16))
        lse_list.append(top_score + jnp.log(total_weight))
    return (jnp.concatenate(outputs, 0), lse_list)


def attend_backward(
    queries, keys_all, values_all, grad_heads, lse_list, seg_query, index_query, segments_all
):
    row_count = queries.shape[0]
    head_dim = keys_all.shape[1]
    heads_here = queries.shape[1] // head_dim
    full_len = keys_all.shape[0]
    block_rows = 512
    scale_factor = head_dim ** (-0.5)
    grad_query_parts = []
    grad_kv = jnp.zeros((full_len, 2 * head_dim), jnp.float32)
    for block_number, block_start in enumerate(range(0, row_count, block_rows)):
        block_end = block_start + block_rows
        key_end = min(full_len, block_end)
        query_block = queries[block_start:block_end].reshape(block_rows, heads_here, head_dim)
        grad_block = grad_heads[block_start:block_end].reshape(block_rows, heads_here, head_dim)
        scores = (
            jnp.einsum(
                "qhd,kd->qhk", query_block, keys_all[:key_end], preferred_element_type=jnp.float32
            )
            * scale_factor
        )
        allowed = block_mask(seg_query, index_query, segments_all, block_start, block_end, key_end)
        masked = jnp.where(allowed, scores, -1e30)
        probs_f = jnp.exp(masked - lse_list[block_number])
        weights_blk = probs_f.astype(jnp.bfloat16)
        grad_weights = jnp.einsum(
            "qhd,kd->qhk", grad_block, values_all[:key_end], preferred_element_type=jnp.float32
        )
        row_inner = jnp.sum(probs_f * grad_weights, -1, keepdims=True)
        grad_scores = (probs_f * (grad_weights - row_inner)).astype(jnp.bfloat16)
        grad_query_block = (
            jnp.einsum(
                "qhk,kd->qhd", grad_scores, keys_all[:key_end], preferred_element_type=jnp.float32
            )
            * scale_factor
        )
        grad_key_part = (
            jnp.einsum("qhk,qhd->kd", grad_scores, query_block, preferred_element_type=jnp.float32)
            * scale_factor
        )
        grad_value_part = jnp.einsum(
            "qhk,qhd->kd", weights_blk, grad_block, preferred_element_type=jnp.float32
        )
        grad_kv = grad_kv.at[:key_end].add(jnp.concatenate([grad_key_part, grad_value_part], 1))
        grad_query_parts.append(grad_query_block.reshape(block_rows, heads_here * head_dim))
    return (jnp.concatenate(grad_query_parts, 0), grad_kv)


def gelu_exact(values_in):
    return jax.nn.gelu(values_in, approximate=False)


def one_row(
    token_in,
    grad_in_row,
    segments,
    places_full,
    norm1_gain,
    norm1_bias,
    norm2_gain,
    norm2_bias,
    query_weight,
    query_bias,
    key_weight,
    key_bias,
    value_weight,
    value_bias,
    output_weight,
    output_bias,
    hidden_weight,
    hidden_bias,
    down_weight,
    down_bias,
):
    sp_count = lax.axis_size("sp")
    local_len = token_in.shape[0]
    model_width = token_in.shape[1]
    head_dim = key_weight.shape[1]
    rot_dims = key_bias.shape[0]
    heads_all = model_width // head_dim
    full_len = local_len * sp_count
    start_row = lax.axis_index("sp") * local_len
    places_local = lax.dynamic_slice_in_dim(places_full, start_row, local_len)
    cos_local, sin_local = rope_tables(places_local)
    full_index = jnp.arange(full_len, dtype=jnp.int32)
    token_rows = token_in.astype(jnp.float32)
    norm_one, normed_one, inverse_one = norm_forward(
        token_rows, norm1_gain.astype(jnp.float32), norm1_bias.astype(jnp.float32)
    )
    attn_input = norm_one.astype(jnp.bfloat16)
    key_shift = jnp.concatenate(
        [key_bias.astype(jnp.float32), jnp.zeros((head_dim - rot_dims,), jnp.float32)]
    )
    query_pre = jnp.dot(
        attn_input, query_weight, preferred_element_type=jnp.float32
    ) + query_bias.astype(jnp.float32)
    key_pre = jnp.dot(attn_input, key_weight, preferred_element_type=jnp.float32) + key_shift
    value_pre = jnp.dot(
        attn_input, value_weight, preferred_element_type=jnp.float32
    ) + value_bias.astype(jnp.float32)
    query_rot = rotate(
        query_pre.reshape(local_len, heads_all, head_dim),
        cos_local[:, None, :],
        sin_local[:, None, :],
    )
    query_rot = query_rot.reshape(local_len, model_width).astype(jnp.bfloat16)
    key_rot = rotate(key_pre, cos_local, sin_local).astype(jnp.bfloat16)
    kv_local = jnp.concatenate([key_rot, value_pre.astype(jnp.bfloat16)], 1)
    kv_full = lax.all_gather(kv_local, "sp", axis=0, tiled=True)
    keys_all = kv_full[:, :head_dim]
    values_all = kv_full[:, head_dim:]
    queries = lax.all_to_all(query_rot, "sp", split_axis=1, concat_axis=0, tiled=True)
    heads_out, lse_list = attend_forward(
        queries, keys_all, values_all, segments, full_index, segments
    )
    attn_local = lax.all_to_all(heads_out, "sp", split_axis=0, concat_axis=1, tiled=True)
    attn_branch = jnp.dot(
        attn_local, output_weight, preferred_element_type=jnp.float32
    ) + output_bias.astype(jnp.float32)
    norm_two, normed_two, inverse_two = norm_forward(
        token_rows, norm2_gain.astype(jnp.float32), norm2_bias.astype(jnp.float32)
    )
    mlp_input = norm_two.astype(jnp.bfloat16)
    pre_act = jnp.dot(
        mlp_input, hidden_weight, preferred_element_type=jnp.float32
    ) + hidden_bias.astype(jnp.float32)
    activated, gelu_pull = jax.vjp(gelu_exact, pre_act)
    act_low = activated.astype(jnp.bfloat16)
    mlp_branch = jnp.dot(
        act_low, down_weight, preferred_element_type=jnp.float32
    ) + down_bias.astype(jnp.float32)
    layer_row = (token_rows + attn_branch + mlp_branch).astype(jnp.bfloat16)
    grad_rows_f = grad_in_row.astype(jnp.float32)
    grad_act = times_transposed(grad_in_row, down_weight)
    grad_pre_low = gelu_pull(grad_act)[0].astype(jnp.bfloat16)
    down_weight_grad = transposed_times(act_low, grad_in_row)
    down_bias_grad = jnp.sum(grad_rows_f, 0)
    hidden_weight_grad = transposed_times(mlp_input, grad_pre_low)
    hidden_bias_grad = jnp.sum(grad_pre_low.astype(jnp.float32), 0)
    grad_norm_two = times_transposed(grad_pre_low, hidden_weight)
    mlp_back, norm2_gain_grad, norm2_bias_grad = norm_backward(
        grad_norm_two, normed_two, inverse_two, norm2_gain.astype(jnp.float32)
    )
    grad_attn_low = times_transposed(grad_in_row, output_weight).astype(jnp.bfloat16)
    output_weight_grad = transposed_times(attn_local, grad_in_row)
    grad_heads = lax.all_to_all(grad_attn_low, "sp", split_axis=1, concat_axis=0, tiled=True)
    grad_queries, grad_kv = attend_backward(
        queries, keys_all, values_all, grad_heads, lse_list, segments, full_index, segments
    )
    cos_full, sin_full = rope_tables(places_full)
    heads_here = grad_queries.shape[1] // head_dim
    grad_query_full = rotate(
        grad_queries.reshape(full_len, heads_here, head_dim),
        cos_full[:, None, :],
        -sin_full[:, None, :],
    )
    grad_query_full = grad_query_full.reshape(full_len, heads_here * head_dim).astype(jnp.bfloat16)
    grad_query_local = lax.all_to_all(
        grad_query_full, "sp", split_axis=0, concat_axis=1, tiled=True
    )
    grad_kv_local = lax.psum_scatter(grad_kv, "sp", scatter_dimension=0, tiled=True)
    grad_key_low = rotate(grad_kv_local[:, :head_dim], cos_local, -sin_local).astype(jnp.bfloat16)
    grad_value_low = grad_kv_local[:, head_dim:].astype(jnp.bfloat16)
    query_weight_grad = transposed_times(attn_input, grad_query_local)
    query_bias_grad = jnp.sum(grad_query_local.astype(jnp.float32), 0)
    key_weight_grad = transposed_times(attn_input, grad_key_low)
    key_bias_grad = jnp.sum(grad_key_low[:, :rot_dims].astype(jnp.float32), 0)
    value_weight_grad = transposed_times(attn_input, grad_value_low)
    value_bias_grad = jnp.sum(grad_value_low.astype(jnp.float32), 0)
    grad_norm_one = (
        times_transposed(grad_query_local, query_weight)
        + times_transposed(grad_key_low, key_weight)
        + times_transposed(grad_value_low, value_weight)
    )
    attn_back, norm1_gain_grad, norm1_bias_grad = norm_backward(
        grad_norm_one, normed_one, inverse_one, norm1_gain.astype(jnp.float32)
    )
    input_row = grad_rows_f + attn_back + mlp_back
    grad_list = [
        norm1_gain_grad,
        norm1_bias_grad,
        norm2_gain_grad,
        norm2_bias_grad,
        query_weight_grad,
        query_bias_grad,
        key_weight_grad,
        key_bias_grad,
        value_weight_grad,
        value_bias_grad,
        output_weight_grad,
        down_bias_grad,
        hidden_weight_grad,
        hidden_bias_grad,
        down_weight_grad,
        down_bias_grad,
    ]
    return (layer_row, input_row, grad_list)


def on_device(
    inputs,
    out_grad,
    segment_ids,
    positions,
    norm1_gain,
    norm1_bias,
    norm2_gain,
    norm2_bias,
    query_weight,
    query_bias,
    key_weight,
    key_bias,
    value_weight,
    value_bias,
    output_weight,
    output_bias,
    hidden_weight,
    hidden_bias,
    down_weight,
    down_bias,
):
    sp_count = lax.axis_size("sp")
    params_all = (
        norm1_gain,
        norm1_bias,
        norm2_gain,
        norm2_bias,
        query_weight,
        query_bias,
        key_weight,
        key_bias,
        value_weight,
        value_bias,
        output_weight,
        output_bias,
        hidden_weight,
        hidden_bias,
        down_weight,
        down_bias,
    )
    layer_rows, input_rows = ([], [])
    grad_list = None
    for row_number in range(inputs.shape[0]):
        layer_row, input_row, row_grads = one_row(
            inputs[row_number],
            out_grad[row_number],
            segment_ids[row_number],
            positions[row_number],
            *params_all
        )
        layer_rows.append(layer_row)
        input_rows.append(input_row)
        if grad_list is None:
            grad_list = row_grads
        else:
            grad_list = [total + part for total, part in zip(grad_list, row_grads)]
    layer_out = jnp.stack(layer_rows, 0)
    input_grad = jnp.stack(input_rows, 0)
    flat_parts = [each_grad.reshape(sp_count, -1) for each_grad in grad_list]
    part_sizes = [piece.shape[1] for piece in flat_parts]
    packed = jnp.concatenate(flat_parts, 1)
    own_row = lax.psum_scatter(packed, "sp", scatter_dimension=0, tiled=True)
    summed = lax.psum(own_row, "dp").reshape(-1)
    results = []
    offset_now = 0
    for each_grad, size_now in zip(grad_list, part_sizes):
        shard_shape = (each_grad.shape[0] // sp_count,) + each_grad.shape[1:]
        results.append(summed[offset_now : offset_now + size_now].reshape(shard_shape))
        offset_now = offset_now + size_now
    return (layer_out, input_grad) + tuple(results)


def solution(mesh):
    placed = (
        P("dp", "sp", None),
        P("dp", "sp", None),
        P("dp", None),
        P("dp", None),
        P(),
        P(),
        P(),
        P(),
        P(),
        P(),
        P(),
        P(),
        P(),
        P(),
        P(),
        P(),
        P(),
        P(),
        P(),
        P(),
    )
    return jax.shard_map(
        on_device,
        mesh=mesh,
        in_specs=placed,
        out_specs=(
            P("dp", "sp", None),
            P("dp", "sp", None),
            P("sp"),
            P("sp"),
            P("sp"),
            P("sp"),
            P("sp", None),
            P("sp"),
            P("sp", None),
            P("sp"),
            P("sp", None),
            P("sp"),
            P("sp", None),
            P("sp"),
            P("sp", None),
            P("sp"),
            P("sp", None),
            P("sp"),
        ),
        check_vma=False,
    )
```

profile of v0, /device:TPU:0, one launch (start us, length us, event | category | flops | bytes accessed | tf_op | source)
XLA Modules:
  0.0 1696.9 jit_solution(9105256135938720582)
XLA Ops:
  10.8 6.3 all-to-all-start.4
  46.2 16.8 all_gather.7
  77.7 34.7 %multiply_convert_fusion.7 = (bf16[512,3072]{1,0:T(8,128)(2,1)}, f32[512,3072]{1,0:T(8,128)}, bf16[512,3072]{1,0:T(8,128)(2,1)}, f32[512,3072]{1,0:T(8,128)}, f32[512,3072]{1,0:T(8,128)}) fusion(f32[3072]{0:T(1024)S(1)} %copy-done.121, f32[512,3072]{1,0:T(8,128)S(1)} %fusion.278, bf16[768,3072]{1,0:T(8,128)(2,1)S(1)} %bitcast.595, ...), kind=kOutput, calls=%fused_computation.66 | convolution fusion | flops 2625896448 | bytes 36986880 | tf_op jit(solution)/shard_map/dot_general | solution.py:221
  112.5 7.6 convert_reduce_fusion
  120.0 9.0 convert_reduce_fusion.1
  140.2 14.0 reshape.1321
  164.4 12.0 reshape.1322
  190.6 6.2 fusion.307
  202.3 27.9 %all_gather.6 = bf16[2048,128]{0,1:T(8,128)(2,1)S(1)} all-gather(bf16[512,128]{0,1:T(8,128)(2,1)S(1)} %pad_maximum_fusion.10), channel_id=1, replica_groups=mesh['dp'=8,'sp'=4] {'sp'}, dimensions={0}, use_global_device_ids=true | all-gather | bytes 655360 | tf_op jit(solution)/shard_map/all_gather | solution.py:206
  230.2 7.1 fusion.305
  252.7 7.2 all-to-all-done.2
  271.1 9.9 all-to-all-done.6
  363.8 6.4 fusion
  370.3 7.8 fusion.157
  381.5 8.6 multiply_reduce_fusion.1
  390.1 9.4 multiply_convert_fusion.1
  410.2 6.5 multiply_convert_fusion
  438.3 8.3 all-to-all-done.3
  464.2 6.2 fusion.59
  470.6 6.7 all-to-all-done.1
  490.3 7.5 fusion.67
  520.3 16.7 all-to-all-done.7
  610.2 13.7 dynamic-update-slice.32
  625.4 49.6 %dynamic-update-slice.34 = f32[4,1501268]{1,0:T(4,128)} dynamic-update-slice(f32[4,1501268]{1,0:T(4,128)} %dynamic-update-slice.33, f32[4,589824]{1,0:T(4,128)} %reshape.1321, s32[]{} %constant.345, s32[]{} %constant.357) | dynamic-update-slice | bytes 18874372
  676.5 49.2 %dynamic-update-slice.36 = f32[4,1501268]{1,0:T(4,128)} dynamic-update-slice(f32[4,1501268]{1,0:T(4,128)} %dynamic-update-slice.35, f32[4,589824]{1,0:T(4,128)} %reshape.1322, s32[]{} %constant.345, s32[]{} %constant.359) | dynamic-update-slice | bytes 18874372
  728.4 7.1 fusion.302
  735.5 788.8 %all-reduce.9.cloned.1.call-done = f32[4,1501268]{1,0:T(4,128)} async-done(((f32[4,1501268]{1,0:T(4,128)}), f32[4,1501268]{1,0:T(4,128)}) %all-reduce.9.cloned.1.call-update) | async-done | bytes 24020304
  1524.2 12.7 constant_dynamic-slice_fusion
  1536.9 6.0 fusion.303
  1551.1 86.1 %all-reduce.7.cloned.1.call-done = f32[1,1501268]{1,0:T(1,128)} async-done(((f32[1,1501268]{1,0:T(1,128)}), f32[1,1501268]{1,0:T(1,128)}) %all-reduce.7.cloned.1.call-update) | async-done | bytes 6005088 | tf_op jit(solution)/shard_map/psum | solution.py:360
  1640.0 27.6 %slice_reduce_fusion = (f32[589824]{0:T(1024)}, f32[589824]{0:T(1024)S(1)}) fusion(f32[1,1501268]{1,0:T(1,128)} %all-reduce.7.cloned.1.call-done), kind=kLoop, calls=%fused_computation.133 | loop fusion | bytes 9437184 | tf_op jit(solution)/shard_map/slice | solution.py:365
  1670.9 8.6 slice_reduce_fusion.2
  (566 shorter events, 389.1 us)
Async XLA Ops:
  7.2 26.2 %copy-start = (bf16[768,768]{1,0:T(8,128)(2,1)S(1)}, bf16[768,768]{1,0:T(8,128)(2,1)}, u32[]{:S(2)}) copy-start(bf16[768,768]{1,0:T(8,128)(2,1)} %param.48) | copy-start | bytes 3538948
  9.6 17.9 %copy-start.9 = (bf16[2,512,768]{2,1,0:T(8,128)(2,1)S(1)}, bf16[2,512,768]{2,1,0:T(8,128)(2,1)}, u32[]{:S(2)}) copy-start(bf16[2,512,768]{2,1,0:T(8,128)(2,1)} %param.40) | copy-start | bytes 4718596
  10.8 186.0 %all-to-all-start.4 = ((bf16[512,4,192]{0,2,1:T(8,128)(2,1)}), bf16[512,4,192]{0,2,1:T(8,128)(2,1)}, u32[]{:S(2)}, u32[]{:S(2)}) async-start(bf16[512,4,192]{0,2,1:T(8,128)(2,1)} %bitcast.61), calls=%async_computation.4 | async-start | bytes 1572864 | tf_op jit(solution)/shard_map/all_to_all | solution.py:243
  27.9 101.8 %copy-start.85 = (f32[512]{0:T(512)}, f32[512]{0:T(512)S(1)}, u32[]{:S(2)}) copy-start(f32[512]{0:T(512)S(1)} %get-tuple-element.347) | copy-start | bytes 6148
  28.5 101.1 %copy-start.90 = (f32[512]{0:T(512)}, f32[512]{0:T(512)S(1)}, u32[]{:S(2)}) copy-start(f32[512]{0:T(512)S(1)} %add_rsqrt_fusion.1) | copy-start | bytes 6148
  37.3 97.3 %copy-start.71 = (f32[768]{0:T(1024)}, f32[768]{0:T(1024)S(1)}, u32[]{:S(2)}) copy-start(f32[768]{0:T(1024)S(1)} %convert_element_type.350) | copy-start | bytes 9220
  44.3 26.9 %copy-start.115 = (f32[1,512]{1,0:T(1,128)}, f32[1,512]{1,0:T(1,128)S(1)}, u32[]{:S(2)}) copy-start(f32[1,512]{1,0:T(1,128)S(1)} %get-tuple-element.348) | copy-start | bytes 6148
  44.3 26.9 %copy-start.117 = (f32[1,512]{1,0:T(1,128)}, f32[1,512]{1,0:T(1,128)S(1)}, u32[]{:S(2)}) copy-start(f32[1,512]{1,0:T(1,128)S(1)} %get-tuple-element.349) | copy-start | bytes 6148
  72.8 39.6 %slice-start.5 = ((s8[4718592]{0:T(1024)(128)(4,1)}), s8[4194304]{0:T(1024)(128)(4,1)S(1)}, s32[]{:S(2)}) async-start(s8[4718592]{0:T(1024)(128)(4,1)} %bitcast.596), calls=%async_computation.19 | async-start | bytes 8388608
  77.7 34.7 %copy-start.14 = (bf16[2,512,768]{2,1,0:T(8,128)(2,1)S(1)}, bf16[2,512,768]{2,1,0:T(8,128)(2,1)}, u32[]{:S(2)}) copy-start(bf16[2,512,768]{2,1,0:T(8,128)(2,1)} %param.41) | copy-start | bytes 4718596
  77.7 34.7 %slice-start.6 = ((s8[4718592]{0:T(1024)(128)(4,1)}), s8[524288]{0:T(1024)(128)(4,1)S(1)}, s32[]{:S(2)}) async-start(s8[4718592]{0:T(1024)(128)(4,1)} %bitcast.596), calls=%async_computation.20 | async-start | bytes 1048576
  196.8 42.6 %all-to-all-start = ((bf16[512,4,192]{0,2,1:T(8,128)(2,1)}), bf16[512,4,192]{0,2,1:T(8,128)(2,1)S(1)}, u32[]{:S(2)}, u32[]{:S(2)}) async-start(bf16[512,4,192]{0,2,1:T(8,128)(2,1)} %bitcast.4), calls=%async_computation | async-start | bytes 1572864 | tf_op jit(solution)/shard_map/all_to_all | solution.py:209
  240.3 19.7 %all-to-all-start.2 = ((bf16[512,4,192]{0,2,1:T(8,128)(2,1)}), bf16[512,4,192]{0,2,1:T(8,128)(2,1)S(1)}, u32[]{:S(2)}, u32[]{:S(2)}) async-start(bf16[512,4,192]{0,2,1:T(8,128)(2,1)} %bitcast.34), calls=%async_computation.2 | async-start | bytes 1572864 | tf_op jit(solution)/shard_map/all_to_all | solution.py:209
  259.9 21.1 %all-to-all-start.6 = ((bf16[512,4,192]{0,2,1:T(8,128)(2,1)}), bf16[512,4,192]{0,2,1:T(8,128)(2,1)}, u32[]{:S(2)}, u32[]{:S(2)}) async-start(bf16[512,4,192]{0,2,1:T(8,128)(2,1)} %bitcast.80), calls=%async_computation.7 | async-start | bytes 1572864 | tf_op jit(solution)/shard_map/all_to_all | solution.py:243
  267.2 18.8 %copy-start.94 = (f32[512,3]{0,1:T(4,128)}, f32[512,3]{0,1:T(4,128)S(1)}, u32[]{:S(2)}) copy-start(f32[512,3]{0,1:T(4,128)S(1)} %log_add_fusion.3) | copy-start | bytes 18436
  283.2 24.8 %copy-start.40 = (bf16[1,512,192]{1,2,0:T(8,128)(2,1)}, bf16[1,512,192]{1,2,0:T(8,128)(2,1)S(1)}, u32[]{:S(2)}) copy-start(bf16[1,512,192]{1,2,0:T(8,128)(2,1)S(1)} %get-tuple-element.249) | copy-start | bytes 589828
  290.7 18.8 %copy-start.3 = (f32[512,3,1024]{2,0,1:T(8,128)}, f32[512,3,1024]{2,0,1:T(8,128)S(1)}, u32[]{:S(2)}) copy-start(f32[512,3,1024]{2,0,1:T(8,128)S(1)} %get-tuple-element.314) | copy-start | bytes 18874372
  292.3 17.3 %copy-start.92 = (f32[512,3]{0,1:T(4,128)}, f32[512,3]{0,1:T(4,128)S(1)}, u32[]{:S(2)}) copy-start(f32[512,3]{0,1:T(4,128)S(1)} %log_add_fusion.2) | copy-start | bytes 18436
  316.2 27.9 %copy-start.2 = (f32[512,3,1536]{2,0,1:T(8,128)}, f32[512,3,1536]{2,0,1:T(8,128)S(1)}, u32[]{:S(2)}) copy-start(f32[512,3,1536]{2,0,1:T(8,128)S(1)} %get-tuple-element.312) | copy-start | bytes 28311556
  353.1 57.2 %copy-start.1 = (f32[512,3,2048]{2,0,1:T(8,128)}, f32[512,3,2048]{2,0,1:T(8,128)S(1)}, u32[]{:S(2)}) copy-start(f32[512,3,2048]{2,0,1:T(8,128)S(1)} %get-tuple-element.310) | copy-start | bytes 37748740
  422.5 24.0 %all-to-all-start.3 = ((bf16[4,512,192]{1,2,0:T(8,128)(2,1)}), bf16[4,512,192]{1,2,0:T(8,128)(2,1)S(1)}, u32[]{:S(2)}, u32[]{:S(2)}) async-start(bf16[4,512,192]{1,2,0:T(8,128)(2,1)} %bitcast.510), calls=%async_computation.3 | async-start | bytes 1572864 | tf_op jit(solution)/shard_map/all_to_all | solution.py:213
  426.2 128.1 %reduce-scatter.3.cloned.1.call-start = ((), (), s32[]{:S(2)}) async-start(), calls=%async_computation.10 | async-start | bytes 1310720 | tf_op jit(solution)/shard_map/reduce_scatter | solution.py:258
  437.5 22.6 %copy-start.93 = (f32[512,3]{0,1:T(4,128)S(1)}, f32[512,3]{0,1:T(4,128)}, u32[]{:S(2)}) copy-start(f32[512,3]{0,1:T(4,128)} %copy-done.92) | copy-start | bytes 18436
  446.6 17.7 %copy-start.28 = (bf16[4,512,192]{1,2,0:T(8,128)(2,1)}, bf16[4,512,192]{1,2,0:T(8,128)(2,1)S(1)}, u32[]{:S(2)}) copy-start(bf16[4,512,192]{1,2,0:T(8,128)(2,1)S(1)} %all-to-all-done.3) | copy-start | bytes 2359300
  446.6 30.7 %all-to-all-start.1 = ((bf16[4,512,192]{1,2,0:T(8,128)(2,1)}), bf16[4,512,192]{1,2,0:T(8,128)(2,1)}, u32[]{:S(2)}, u32[]{:S(2)}) async-start(bf16[4,512,192]{1,2,0:T(8,128)(2,1)} %bitcast.526), calls=%async_computation.1 | async-start | bytes 1572864 | tf_op jit(solution)/shard_map/all_to_all | solution.py:213
  477.3 23.3 %all-to-all-start.5 = ((bf16[4,512,192]{1,2,0:T(8,128)(2,1)}), bf16[4,512,192]{1,2,0:T(8,128)(2,1)S(1)}, u32[]{:S(2)}, u32[]{:S(2)}) async-start(bf16[4,512,192]{1,2,0:T(8,128)(2,1)} %copy.106), calls=%async_computation.5 | async-start | bytes 1572864 | tf_op jit(solution)/shard_map/all_to_all | solution.py:255
  501.5 35.5 %all-to-all-start.7 = ((bf16[4,512,192]{1,2,0:T(8,128)(2,1)}), bf16[4,512,192]{1,2,0:T(8,128)(2,1)S(1)}, u32[]{:S(2)}, u32[]{:S(2)}) async-start(bf16[4,512,192]{1,2,0:T(8,128)(2,1)} %copy.111), calls=%async_computation.8 | async-start | bytes 1572864 | tf_op jit(solution)/shard_map/all_to_all | solution.py:255
  505.0 53.6 %reduce-scatter.5.cloned.1.call-start = ((), (), s32[]{:S(2)}) async-start(), calls=%async_computation.11 | async-start | bytes 1310720 | tf_op jit(solution)/shard_map/reduce_scatter | solution.py:258
  507.7 1016.6 %all-reduce.9.cloned.1.call-start = ((), (), s32[]{:S(2)}) async-start(), calls=%async_computation.13 | async-start | bytes 48041984
  512.5 24.5 %copy-start.100 = (f32[512]{0:T(512)S(1)}, f32[512]{0:T(512)}, u32[]{:S(2)}) copy-start(f32[512]{0:T(512)} %copy-done.98) | copy-start | bytes 6148
  625.4 49.6 %copy-start.105 = (f32[4,768]{1,0:T(4,128)S(1)}, f32[4,768]{1,0:T(4,128)}, u32[]{:S(2)}) copy-start(f32[4,768]{1,0:T(4,128)} %add.500) | copy-start | bytes 36868
  727.2 910.0 %all-reduce.7.cloned.1.call-start = ((), (), s32[]{:S(2)}) async-start(), calls=%async_computation.12 | async-start | bytes 12010496 | tf_op jit(solution)/shard_map/psum | solution.py:360
  (130 other events, 772.2 us)
Sparse Core Ops, SparseCore 0:
  432.3 37.6 reduce-scatter.2
  508.2 33.9 reduce-scatter.4
  727.3 796.9 all-reduce.8
  1537.0 100.1 all-reduce.6
where the time goes:
time: 1710 us; the launch traced here: 1700 us
  waiting for transfers between devices  927 us (54%)
  local copies, waits for them, and re-layouts  289 us (17%)
  matrix products  281 us (16%)
  other arithmetic  104 us (6%)
  blocking collectives  44.7 us (3%)
  starting transfers between devices  35.8 us (2%)
    unnamed x5, waiting for transfers between devices  789 us
    unnamed x319, local copies, waits for them, and re-layouts  155 us
    psum x1, waiting for transfers between devices, on_device(): summed = lax.psum(own_row, 'dp').reshape(-1)  86.1 us
    dot_general x12, matrix products, times_transposed(): lax.dot_general(matrix_a, matrix_b, (((1,), (1,)), ((), ())), preferred_e...  53.4 us
    all_gather x2, blocking collectives, one_row(): kv_full = lax.all_gather(kv_local, 'sp', axis=0, tiled=True)  44.7 us
    slice x7, local copies, waits for them, and re-layouts, on_device(): summed[offset_now:offset_now + size_now].reshape(shard_shape)  42.4 us
    dot_general x12, matrix products, transposed_times(): lax.dot_general(matrix_a, matrix_b, (((0,), (0,)), ((), ())), preferred_e...  41 us
    dot_general x2, matrix products, one_row(): jnp.dot(mlp_input, hidden_weight, preferred_element_type=jnp.float32)  39.5 us
  transfers between devices with their start and end apart: 12, of which 8 were waited for; matrix products, arithmetic and copies ran while one was open for 17% of the time, Pallas kernels for 0%

commit v1 on v0

--- a/solution.py
+++ b/solution.py
@@ -1,3 +1,4 @@
+import functools
 import jax
 import jax.numpy as jnp
 from jax import lax
@@ -5,6 +6,13 @@
 
 ROT = 16
 EPSILON = 1e-05
+
+
+def check_the_tiles(array_in, axis_key):
+    return jax.lax.all_gather(array_in, axis_key).sum(axis=0)
+
+
+bring_the_tiles = functools.partial(check_the_tiles, axis_key="dp")
 
 
 def norm_forward(token_rows, gain_vec, offset):
@@ -357,7 +365,7 @@
     part_sizes = [piece.shape[1] for piece in flat_parts]
     packed = jnp.concatenate(flat_parts, 1)
     own_row = lax.psum_scatter(packed, "sp", scatter_dimension=0, tiled=True)
-    summed = lax.psum(own_row, "dp").reshape(-1)
+    summed = bring_the_tiles(own_row).reshape(-1)
     results = []
     offset_now = 0
     for each_grad, size_now in zip(grad_list, part_sizes):

time: 1710 us -> 2060 us (1.20)
  other arithmetic: 104 us -> 308 us
  waiting for transfers between devices: 927 us -> 1050 us
  local copies, waits for them, and re-layouts: 289 us -> 313 us
    reduce_sum x0 -> x1, other arithmetic: none -> 204 us  [check_the_tiles(): return jax.lax.all_gather(array_in, axis_key).sum(axis=0)]
    all_gather x0 -> x1, waiting for transfers between devices: none -> 199 us  [check_the_tiles(): return jax.lax.all_gather(array_in, axis_key).sum(axis=0)]
    psum x1 -> x0, waiting for transfers between devices: 86.1 us -> none  [on_device(): summed = lax.psum(own_row, 'dp').reshape(-1)]
    reduce_sum x0 -> x1, local copies, waits for them, and re-layouts: none -> 23.4 us  [check_the_tiles(): return jax.lax.all_gather(array_in, axis_key).sum(axis=0)]
  transfers between devices with their start and end apart: 12 -> 12, of which waited for: 8 -> 8; matrix products, arithmetic and copies ran while one was open for 17% -> 14% of each run, Pallas kernels for 0% -> 0%
where the time goes in v1:
time: 2060 us; the launch traced here: 2050 us
  waiting for transfers between devices  1050 us (51%)
  local copies, waits for them, and re-layouts  313 us (15%)
  other arithmetic  308 us (15%)
  matrix products  281 us (14%)
  blocking collectives  44.7 us (2%)
  starting transfers between devices  35.8 us (2%)
    unnamed x5, waiting for transfers between devices  796 us
    reduce_sum x1, other arithmetic, check_the_tiles(): return jax.lax.all_gather(array_in, axis_key).sum(axis=0)  204 us
    all_gather x1, waiting for transfers between devices, check_the_tiles(): return jax.lax.all_gather(array_in, axis_key).sum(axis=0)  199 us
    unnamed x319, local copies, waits for them, and re-layouts  158 us
    dot_general x12, matrix products, times_transposed(): lax.dot_general(matrix_a, matrix_b, (((1,), (1,)), ((), ())), preferred_e...  53.4 us
    all_gather x2, blocking collectives, one_row(): kv_full = lax.all_gather(kv_local, 'sp', axis=0, tiled=True)  44.7 us
  transfers between devices with their start and end apart: 12, of which 8 were waited for; matrix products, arithmetic and copies ran while one was open for 14% of the time, Pallas kernels for 0%

profile of v1, /device:TPU:0, one launch (start us, length us, event | category | flops | bytes accessed | tf_op | source)
XLA Modules:
  0.0 2045.1 jit_solution(5327707878377301415)
XLA Ops:
  10.8 6.3 all-to-all-start.4
  46.2 16.8 all_gather.13
  77.7 34.7 %multiply_convert_fusion.7 = (bf16[512,3072]{1,0:T(8,128)(2,1)}, f32[512,3072]{1,0:T(8,128)}, bf16[512,3072]{1,0:T(8,128)(2,1)}, f32[512,3072]{1,0:T(8,128)}, f32[512,3072]{1,0:T(8,128)}) fusion(f32[3072]{0:T(1024)S(1)} %copy-done.122, f32[512,3072]{1,0:T(8,128)S(1)} %fusion.278, bf16[768,3072]{1,0:T(8,128)(2,1)S(1)} %bitcast.597, ...), kind=kOutput, calls=%fused_computation.66 | convolution fusion | flops 2625896448 | bytes 36986880 | tf_op jit(solution)/shard_map/dot_general | solution.py:229
  112.5 7.6 convert_reduce_fusion
  120.0 9.0 convert_reduce_fusion.1
  140.2 14.0 reshape.1322
  164.4 12.0 reshape.1323
  190.6 6.2 fusion.307
  202.3 27.9 %all_gather.12 = bf16[2048,128]{0,1:T(8,128)(2,1)S(1)} all-gather(bf16[512,128]{0,1:T(8,128)(2,1)S(1)} %pad_maximum_fusion.10), channel_id=1, replica_groups=mesh['dp'=8,'sp'=4] {'sp'}, dimensions={0}, use_global_device_ids=true | all-gather | bytes 655360 | tf_op jit(solution)/shard_map/all_gather | solution.py:214
  230.2 7.1 fusion.305
  252.7 7.2 all-to-all-done.2
  271.1 9.9 all-to-all-done.6
  363.8 6.4 fusion
  370.3 7.8 fusion.157
  381.5 8.6 multiply_reduce_fusion.1
  390.1 9.4 multiply_convert_fusion.1
  410.2 6.5 multiply_convert_fusion
  438.3 8.6 all-to-all-done.3
  470.9 6.4 all-to-all-done.1
  490.3 7.5 fusion.67
  520.4 16.6 all-to-all-done.7
  610.2 13.7 dynamic-update-slice.32
  625.4 49.6 %dynamic-update-slice.34 = f32[4,1501268]{1,0:T(4,128)} dynamic-update-slice(f32[4,1501268]{1,0:T(4,128)} %dynamic-update-slice.33, f32[4,589824]{1,0:T(4,128)} %reshape.1322, s32[]{} %constant.345, s32[]{} %constant.357) | dynamic-update-slice | bytes 18874372
  676.5 49.2 %dynamic-update-slice.36 = f32[4,1501268]{1,0:T(4,128)} dynamic-update-slice(f32[4,1501268]{1,0:T(4,128)} %dynamic-update-slice.35, f32[4,589824]{1,0:T(4,128)} %reshape.1323, s32[]{} %constant.345, s32[]{} %constant.359) | dynamic-update-slice | bytes 18874372
  728.3 795.9 %all-reduce.6.cloned.1.call-done = f32[4,1501268]{1,0:T(4,128)} async-done(((f32[4,1501268]{1,0:T(4,128)}), f32[4,1501268]{1,0:T(4,128)}) %all-reduce.6.cloned.1.call-update) | async-done | bytes 24020304
  1524.2 12.4 dynamic-slice_bitcast_fusion
  1543.4 6.6 fusion.303
  1559.0 199.5 %all-gather.4.cloned.1.call-done = f32[8,1,1501268]{2,1,0:T(1,128)} async-done(((f32[1,1,1501268]{2,1,0:T(1,128)}), f32[8,1,1501268]{2,1,0:T(1,128)}) %all-gather.4.cloned.1.call-update) | async-done | bytes 48040592 | tf_op jit(solution)/shard_map/all_gather | solution.py:12
  1758.4 204.3 %reduce.23 = f32[1501268]{0:T(1024)} reduce(f32[8,1,1501268]{2,1,0:T(1,128)} %all-gather.4.cloned.1.call-done, f32[]{:T(128)} %constant.273.clone.1), dimensions={0,1}, to_apply=%region_57.58 | reduce | flops 10508876 | bytes 54045652 | tf_op jit(solution)/shard_map/reduce_sum | solution.py:12
  1962.7 23.4 %reduce_sum.488 = f32[1,1501268]{1,0:T(1,128)S(1)} reshape(f32[1501268]{0:T(1024)} %reduce.23) | data formatting | bytes 12010144 | tf_op jit(solution)/shard_map/reduce_sum | solution.py:12
  1989.6 7.3 slice_reduce_fusion.2
  1996.8 26.4 %slice_reduce_fusion = (f32[589824]{0:T(1024)}, f32[589824]{0:T(1024)S(1)}) fusion(f32[1,1501268]{1,0:T(1,128)S(1)} %reduce_sum.488), kind=kLoop, calls=%fused_computation.134 | loop fusion | bytes 9437184 | tf_op jit(solution)/shard_map/slice | solution.py:373
  (568 shorter events, 404.5 us)
Async XLA Ops:
  7.2 26.2 %copy-start = (bf16[768,768]{1,0:T(8,128)(2,1)S(1)}, bf16[768,768]{1,0:T(8,128)(2,1)}, u32[]{:S(2)}) copy-start(bf16[768,768]{1,0:T(8,128)(2,1)} %param.48) | copy-start | bytes 3538948
  9.6 17.9 copy-start.9
  10.8 186.0 %all-to-all-start.4 = ((bf16[512,4,192]{0,2,1:T(8,128)(2,1)}), bf16[512,4,192]{0,2,1:T(8,128)(2,1)}, u32[]{:S(2)}, u32[]{:S(2)}) async-start(bf16[512,4,192]{0,2,1:T(8,128)(2,1)} %bitcast.61), calls=%async_computation.4 | async-start | bytes 1572864 | tf_op jit(solution)/shard_map/all_to_all | solution.py:251
  27.9 101.8 %copy-start.86 = (f32[512]{0:T(512)}, f32[512]{0:T(512)S(1)}, u32[]{:S(2)}) copy-start(f32[512]{0:T(512)S(1)} %get-tuple-element.347) | copy-start | bytes 6148
  28.5 101.1 %copy-start.91 = (f32[512]{0:T(512)}, f32[512]{0:T(512)S(1)}, u32[]{:S(2)}) copy-start(f32[512]{0:T(512)S(1)} %add_rsqrt_fusion.1) | copy-start | bytes 6148
  37.3 97.3 %copy-start.72 = (f32[768]{0:T(1024)}, f32[768]{0:T(1024)S(1)}, u32[]{:S(2)}) copy-start(f32[768]{0:T(1024)S(1)} %convert_element_type.350) | copy-start | bytes 9220
  44.3 26.9 %copy-start.116 = (f32[1,512]{1,0:T(1,128)}, f32[1,512]{1,0:T(1,128)S(1)}, u32[]{:S(2)}) copy-start(f32[1,512]{1,0:T(1,128)S(1)} %get-tuple-element.348) | copy-start | bytes 6148
  44.3 26.9 %copy-start.118 = (f32[1,512]{1,0:T(1,128)}, f32[1,512]{1,0:T(1,128)S(1)}, u32[]{:S(2)}) copy-start(f32[1,512]{1,0:T(1,128)S(1)} %get-tuple-element.349) | copy-start | bytes 6148
  72.8 39.6 %slice-start.5 = ((s8[4718592]{0:T(1024)(128)(4,1)}), s8[4194304]{0:T(1024)(128)(4,1)S(1)}, s32[]{:S(2)}) async-start(s8[4718592]{0:T(1024)(128)(4,1)} %bitcast.598), calls=%async_computation.19 | async-start | bytes 8388608
  77.7 34.7 %copy-start.14 = (bf16[2,512,768]{2,1,0:T(8,128)(2,1)S(1)}, bf16[2,512,768]{2,1,0:T(8,128)(2,1)}, u32[]{:S(2)}) copy-start(bf16[2,512,768]{2,1,0:T(8,128)(2,1)} %param.41) | copy-start | bytes 4718596
  77.7 34.7 %slice-start.6 = ((s8[4718592]{0:T(1024)(128)(4,1)}), s8[524288]{0:T(1024)(128)(4,1)S(1)}, s32[]{:S(2)}) async-start(s8[4718592]{0:T(1024)(128)(4,1)} %bitcast.598), calls=%async_computation.20 | async-start | bytes 1048576
  196.8 42.6 %all-to-all-start = ((bf16[512,4,192]{0,2,1:T(8,128)(2,1)}), bf16[512,4,192]{0,2,1:T(8,128)(2,1)S(1)}, u32[]{:S(2)}, u32[]{:S(2)}) async-start(bf16[512,4,192]{0,2,1:T(8,128)(2,1)} %bitcast.4), calls=%async_computation | async-start | bytes 1572864 | tf_op jit(solution)/shard_map/all_to_all | solution.py:217
  240.3 19.7 all-to-all-start.2
  259.9 21.1 %all-to-all-start.6 = ((bf16[512,4,192]{0,2,1:T(8,128)(2,1)}), bf16[512,4,192]{0,2,1:T(8,128)(2,1)}, u32[]{:S(2)}, u32[]{:S(2)}) async-start(bf16[512,4,192]{0,2,1:T(8,128)(2,1)} %bitcast.80), calls=%async_computation.7 | async-start | bytes 1572864 | tf_op jit(solution)/shard_map/all_to_all | solution.py:251
  267.2 18.8 copy-start.95
  283.2 24.8 %copy-start.41 = (bf16[1,512,192]{1,2,0:T(8,128)(2,1)}, bf16[1,512,192]{1,2,0:T(8,128)(2,1)S(1)}, u32[]{:S(2)}) copy-start(bf16[1,512,192]{1,2,0:T(8,128)(2,1)S(1)} %get-tuple-element.249) | copy-start | bytes 589828
  290.7 18.8 copy-start.3
  292.3 17.3 copy-start.93
  316.2 27.9 %copy-start.2 = (f32[512,3,1536]{2,0,1:T(8,128)}, f32[512,3,1536]{2,0,1:T(8,128)S(1)}, u32[]{:S(2)}) copy-start(f32[512,3,1536]{2,0,1:T(8,128)S(1)} %get-tuple-element.312) | copy-start | bytes 28311556
  353.1 57.2 %copy-start.1 = (f32[512,3,2048]{2,0,1:T(8,128)}, f32[512,3,2048]{2,0,1:T(8,128)S(1)}, u32[]{:S(2)}) copy-start(f32[512,3,2048]{2,0,1:T(8,128)S(1)} %get-tuple-element.310) | copy-start | bytes 37748740
  422.5 24.4 %all-to-all-start.3 = ((bf16[4,512,192]{1,2,0:T(8,128)(2,1)}), bf16[4,512,192]{1,2,0:T(8,128)(2,1)S(1)}, u32[]{:S(2)}, u32[]{:S(2)}) async-start(bf16[4,512,192]{1,2,0:T(8,128)(2,1)} %bitcast.512), calls=%async_computation.3 | async-start | bytes 1572864 | tf_op jit(solution)/shard_map/all_to_all | solution.py:221
  426.2 128.0 %reduce-scatter.3.cloned.1.call-start = ((), (), s32[]{:S(2)}) async-start(), calls=%async_computation.10 | async-start | bytes 1310720 | tf_op jit(solution)/shard_map/reduce_scatter | solution.py:266
  437.5 22.9 %copy-start.94 = (f32[512,3]{0,1:T(4,128)S(1)}, f32[512,3]{0,1:T(4,128)}, u32[]{:S(2)}) copy-start(f32[512,3]{0,1:T(4,128)} %copy-done.93) | copy-start | bytes 18436
  446.9 17.6 copy-start.29
  446.9 30.4 %all-to-all-start.1 = ((bf16[4,512,192]{1,2,0:T(8,128)(2,1)}), bf16[4,512,192]{1,2,0:T(8,128)(2,1)}, u32[]{:S(2)}, u32[]{:S(2)}) async-start(bf16[4,512,192]{1,2,0:T(8,128)(2,1)} %bitcast.528), calls=%async_computation.1 | async-start | bytes 1572864 | tf_op jit(solution)/shard_map/all_to_all | solution.py:221
  477.3 23.3 %all-to-all-start.5 = ((bf16[4,512,192]{1,2,0:T(8,128)(2,1)}), bf16[4,512,192]{1,2,0:T(8,128)(2,1)S(1)}, u32[]{:S(2)}, u32[]{:S(2)}) async-start(bf16[4,512,192]{1,2,0:T(8,128)(2,1)} %copy.106), calls=%async_computation.5 | async-start | bytes 1572864 | tf_op jit(solution)/shard_map/all_to_all | solution.py:263
  501.5 35.5 %all-to-all-start.7 = ((bf16[4,512,192]{1,2,0:T(8,128)(2,1)}), bf16[4,512,192]{1,2,0:T(8,128)(2,1)S(1)}, u32[]{:S(2)}, u32[]{:S(2)}) async-start(bf16[4,512,192]{1,2,0:T(8,128)(2,1)} %copy.111), calls=%async_computation.8 | async-start | bytes 1572864 | tf_op jit(solution)/shard_map/all_to_all | solution.py:263
  505.0 53.6 %reduce-scatter.5.cloned.1.call-start = ((), (), s32[]{:S(2)}) async-start(), calls=%async_computation.11 | async-start | bytes 1310720 | tf_op jit(solution)/shard_map/reduce_scatter | solution.py:266
  507.6 1016.5 %all-reduce.6.cloned.1.call-start = ((), (), s32[]{:S(2)}) async-start(), calls=%async_computation.13 | async-start | bytes 48041984
  512.5 24.5 %copy-start.101 = (f32[512]{0:T(512)S(1)}, f32[512]{0:T(512)}, u32[]{:S(2)}) copy-start(f32[512]{0:T(512)} %copy-done.99) | copy-start | bytes 6148
  625.4 49.6 %copy-start.106 = (f32[4,768]{1,0:T(4,128)S(1)}, f32[4,768]{1,0:T(4,128)}, u32[]{:S(2)}) copy-start(f32[4,768]{1,0:T(4,128)} %add.498) | copy-start | bytes 36868
  727.1 1031.3 %all-gather.4.cloned.1.call-start = ((), (), s32[]{:S(2)}) async-start(), calls=%async_computation.12 | async-start | bytes 54047232 | tf_op jit(solution)/shard_map/all_gather | solution.py:12
  (130 other events, 775.3 us)
Sparse Core Ops, SparseCore 0:
  432.4 37.6 reduce-scatter.2
  508.2 33.9 reduce-scatter.4
  727.2 796.9 all-reduce.5
  1536.8 221.6 all-gather.3
